TPU v7x, 256 devices: a whole 4x4x8 slice. The times are simulated.
256 devices in a mesh: shard: 64 (over z, y, core), help: 4 (over x).
Axes of the slice: x: 4, y: 4, z: 8, core: 2. Of those that a mesh axis runs over, the one named last changes fastest.
Arguments:
- queries: bfloat16 [65536, 768], P(('shard', 'help')), may hold values from -6 to 6
- probe_group: int32 [65536, 2], P(('shard', 'help')), may hold values from 0 to 63, all different within a row; in each aligned block of 256 rows (0 to 255, 256 to 511, ...) at most 16 rows name the same one
- probe_local: int32 [65536, 2], P(('shard', 'help')), may hold values from 0 to 3
- points: bfloat16 [262144, 768], P(('shard', 'help')), may hold values from -6 to 6
- point_cluster: int32 [64, 4096], P('shard'), may hold values from 0 to 3, never falling along the last dimension, each value on 1 to 3072 neighbouring positions
- test_matrix: bfloat16 [32, 262144], P(None, ('shard', 'help')), may hold values from -6 to 6
Outputs:
- sketch: float32 [32, 262144], P(None, ('shard', 'help'))
- regressor: float32 [256, 32, 768], P(('shard', 'help'))
Inputs may be any that keep to these rules, and one draw needn't show every extreme that they name: `probe_group`: A query's 2 groups differ. Among the 256 queries of one device (aligned blocks of rows), at most 16 pairs (q,k) name one group, and in some blocks one group is named exactly 16 times.
All inputs are finite; a program needn't handle non-finite values.
Results may differ from a plain program's by a relative error of at most 0.0037.
Values may be sent and summed in bfloat16 or wider, within the bound.
A program may use at most 64 MiB of HBM per device.

v0:
```python
import jax
import jax.numpy as jnp
from jax import lax
from jax.sharding import PartitionSpec as P

F32 = jnp.float32
BF16 = jnp.bfloat16


def split(v):
    hi = v.astype(BF16)
    lo = (v - hi.astype(F32)).astype(BF16)
    return (hi, lo)


def dot2(v, w, dims):
    hi, lo = split(v)
    return lax.dot_general(hi, w, (dims, ((), ())), preferred_element_type=F32) + lax.dot_general(
        lo, w, (dims, ((), ())), preferred_element_type=F32
    )


def shards(queries, probe_group, probe_local, points, point_cluster, test_matrix):
    groups = lax.axis_size("shard")
    helpers = lax.axis_size("help")
    helper = lax.axis_index("help")
    rows, width = queries.shape
    probes = probe_group.shape[1]
    capacity = 2 * rows * probes // groups
    slots = groups * capacity
    rank = test_matrix.shape[0]
    own_points = points.shape[0]
    clusters = helpers
    scale = width ** (-0.5)
    target = probe_group.reshape(-1)
    hot = (target[:, None] == jnp.arange(groups, dtype=jnp.int32)[None, :]).astype(BF16)
    pairs = rows * probes
    before = (
        jnp.arange(pairs, dtype=jnp.int32)[:, None] > jnp.arange(pairs, dtype=jnp.int32)[None, :]
    ).astype(BF16)
    counts = jnp.dot(before, hot, preferred_element_type=F32)
    place = target * capacity + jnp.sum(counts * hot.astype(F32), axis=1).astype(jnp.int32)
    place = place.reshape(rows, probes)
    slot = jnp.arange(slots, dtype=jnp.int32)
    hit = [slot[:, None] == place[:, k][None, :] for k in range(probes)]
    packed = jnp.dot((hit[0] | hit[1]).astype(BF16), queries, preferred_element_type=F32).astype(
        BF16
    )
    ids = -1 + sum(
        (
            jnp.sum(jnp.where(hit[k], probe_local[:, k][None, :] + 1, 0), axis=1)
            for k in range(probes)
        )
    )
    pool = lax.all_to_all(
        packed.reshape(groups, capacity, width), "shard", split_axis=0, concat_axis=0, tiled=True
    ).reshape(slots, width)
    pool_ids = lax.all_to_all(
        ids.astype(jnp.int32).reshape(groups, 1, capacity),
        "shard",
        split_axis=0,
        concat_axis=0,
        tiled=True,
    ).reshape(slots)
    group_ids = point_cluster[0]
    own_ids = lax.dynamic_slice_in_dim(group_ids, helper * own_points, own_points, 0)
    labels = jnp.arange(clusters, dtype=jnp.int32)
    resident = jnp.sum((group_ids[None, :] == labels[:, None]).astype(F32), axis=1)
    own_hot = own_ids[None, :] == labels[:, None]
    spread = jnp.where(own_hot[:, None, :], test_matrix[None], 0).reshape(
        clusters * rank, own_points
    )
    lead = lax.psum(jnp.dot(spread, points, preferred_element_type=F32), "help")
    lifted = dot2(lead * scale, pool, ((1,), (1,)))
    pool_hot = pool_ids[None, :] == labels[:, None]
    lifted = jnp.where(pool_hot[:, None, :], lifted.reshape(clusters, rank, slots), 0.0).reshape(
        clusters * rank, slots
    )
    back = dot2(lifted * scale, pool, ((1,), (0,)))
    named = jnp.sum(pool_hot.astype(F32), axis=1)
    back, queried = lax.psum((back, named), "help")
    product = dot2(back, points, ((1,), (1,))).reshape(clusters, rank, own_points)
    factor = 1.0 / jnp.sqrt((queried + 1.0) * (queried + resident))
    sketch = jnp.sum(jnp.where(own_hot[:, None, :], product * factor[:, None, None], 0.0), axis=0)
    rounded = sketch.astype(BF16)
    weighted = jnp.where(own_hot[:, None, :], rounded[None], 0).reshape(clusters * rank, own_points)
    summed = jnp.dot(weighted, points, preferred_element_type=F32)
    own = lax.psum_scatter(
        summed.reshape(clusters, rank, width), "help", scatter_dimension=0, tiled=True
    )
    own_scale = lax.dynamic_slice_in_dim(1.0 / jnp.sqrt(resident), helper, 1, 0)
    return (sketch, own * own_scale[:, None, None])


def solution(mesh):
    in_specs = (
        P(("shard", "help"), None),
        P(("shard", "help"), None),
        P(("shard", "help"), None),
        P(("shard", "help"), None),
        P("shard", None),
        P(None, ("shard", "help")),
    )
    out_specs = (P(None, ("shard", "help")), P(("shard", "help"), None, None))
    return jax.shard_map(shards, mesh=mesh, in_specs=in_specs, out_specs=out_specs, check_vma=False)
```

profile of v0, /device:TPU:8, one launch (start us, length us, event | category | flops | bytes accessed | tf_op | source)
XLA Modules:
  0.0 178.3 jit_solution(8546420351986458754)
XLA Ops:
  7.2 0.9 copy.22
  8.1 0.1 eq.103
  8.3 0.3 fusion.4
  8.6 0.1 convert_element_type.64
  8.8 0.7 multiply_add_fusion
  9.5 0.8 slice_add_fusion
  10.3 0.3 select_reduce_fusion
  10.6 0.7 add.91
  11.3 12.1 %all-to-all-start = ((s32[64,1,16]{2,1,0:T(1,128)}), s32[64,1,16]{2,1,0:T(1,128)S(1)}, u32[]{:S(2)}, u32[]{:S(2)}) async-start(s32[64,1,16]{2,1,0:T(1,128)} %bitcast.5), calls=%async_computation | async-start | bytes 65536 | tf_op jit(solution)/shard_map/all_to_all | solution.py:58
  23.4 2.8 %convolution_convert_fusion = bf16[1024,768]{1,0:T(8,128)(2,1)} fusion(bf16[256,768]{1,0:T(8,128)(2,1)} %param.6, s32[256]{0:T(256)S(1)} %bitcast.38, s32[256]{0:T(256)S(1)} %bitcast.36), kind=kOutput, calls=%fused_computation | convolution fusion | flops 404226048 | bytes 1968128 | tf_op jit(solution)/shard_map/dot_general | solution.py:46
  26.2 5.8 %all-to-all-done = s32[64,1,16]{2,1,0:T(1,128)S(1)} async-done(((s32[64,1,16]{2,1,0:T(1,128)}), s32[64,1,16]{2,1,0:T(1,128)S(1)}, u32[]{:S(2)}, u32[]{:S(2)}) %all-to-all-start) | async-done | bytes 4128 | tf_op jit(solution)/shard_map/all_to_all | solution.py:58
  32.0 5.7 %all-to-all-start.1 = ((bf16[64,16,768]{2,1,0:T(8,128)(2,1)}), bf16[64,16,768]{2,1,0:T(8,128)(2,1)S(1)}, u32[]{:S(2)}, u32[]{:S(2)}) async-start(bf16[64,16,768]{2,1,0:T(8,128)(2,1)} %bitcast.30), calls=%async_computation.1 | async-start | bytes 3145728 | tf_op jit(solution)/shard_map/all_to_all | solution.py:55
  37.7 0.7 constant_dynamic-slice_fusion
  38.5 1.2 fusion.29
  39.7 0.5 broadcast.69
  40.2 0.7 reduce.3
  41.1 0.1 convert_reduce_fusion.1
  41.2 48.3 %all-reduce.3.cloned.1.call-done = f32[128,768]{1,0:T(8,128)} async-done(((f32[128,768]{1,0:T(8,128)}), f32[128,768]{1,0:T(8,128)}) %all-reduce.3.cloned.1.call-update) | async-done | bytes 393232 | tf_op jit(solution)/shard_map/psum | solution.py:73
  89.5 1.7 fusion.9
  91.3 0.7 fusion.3
  91.9 0.4 fusion.16
  92.4 1.1 convolution_add_fusion.2
  93.6 0.1 convert_reduce_fusion
  93.7 9.3 %psum.23 = f32[4]{0:T(128)S(1)} all-reduce(f32[4]{0:T(128)S(1)} %get-tuple-element.2), channel_id=1, replica_groups=mesh['shard'=64,'help'=4] {'help'}, use_global_device_ids=true, to_apply=%region_6.7 | all-reduce | flops 4 | bytes 32 | tf_op jit(solution)/shard_map/psum | solution.py:81
  103.1 38.5 %all-reduce.5.cloned.1.call-done = f32[128,768]{1,0:T(8,128)} async-done(((f32[128,768]{1,0:T(8,128)}), f32[128,768]{1,0:T(8,128)}) %all-reduce.5.cloned.1.call-update) | async-done | bytes 393232 | tf_op jit(solution)/shard_map/psum | solution.py:81
  141.6 1.7 fusion.21
  143.3 0.7 convolution_add_fusion
  144.0 0.1 select_reduce_fusion.2
  144.1 1.1 fusion
  145.3 0.6 dynamic_slice.7
  145.9 23.7 %reduce-scatter.2.cloned.1.call-done = f32[1,32,768]{2,1,0:T(8,128)} async-done(((f32[4,32,768]{2,1,0:T(8,128)}), f32[1,32,768]{2,1,0:T(8,128)}) %reduce-scatter.2.cloned.1.call-update) | async-done | bytes 98320 | tf_op jit(solution)/shard_map/reduce_scatter | solution.py:88
  169.6 2.2 %broadcast_multiply_fusion = f32[1,32,768]{2,1,0:T(8,128)} fusion(f32[1,32,768]{2,1,0:T(8,128)} %reduce-scatter.2.cloned.1.call-done, f32[]{:T(128)} %bitcast.13), kind=kLoop, calls=%fused_computation.42 | loop fusion | flops 24576 | bytes 196612 | tf_op jit(solution)/shard_map/mul | solution.py:92
  (29 shorter events, 0.5 us)
Async XLA Ops:
  7.2 31.3 %copy-start = (bf16[1024,768]{1,0:T(8,128)(2,1)S(1)}, bf16[1024,768]{1,0:T(8,128)(2,1)}, u32[]{:S(2)}) copy-start(bf16[1024,768]{1,0:T(8,128)(2,1)} %param.9) | copy-start | bytes 4718596
  11.3 20.7 %all-to-all-start = ((s32[64,1,16]{2,1,0:T(1,128)}), s32[64,1,16]{2,1,0:T(1,128)S(1)}, u32[]{:S(2)}, u32[]{:S(2)}) async-start(s32[64,1,16]{2,1,0:T(1,128)} %bitcast.5), calls=%async_computation | async-start | bytes 65536 | tf_op jit(solution)/shard_map/all_to_all | solution.py:58
  32.0 6.5 %copy-start.4 = (bf16[32,1024]{1,0:T(8,128)(2,1)S(1)}, bf16[32,1024]{1,0:T(8,128)(2,1)}, u32[]{:S(2)}) copy-start(bf16[32,1024]{1,0:T(8,128)(2,1)} %param.11) | copy-start | bytes 196612
  32.0 57.5 %all-to-all-start.1 = ((bf16[64,16,768]{2,1,0:T(8,128)(2,1)}), bf16[64,16,768]{2,1,0:T(8,128)(2,1)S(1)}, u32[]{:S(2)}, u32[]{:S(2)}) async-start(bf16[64,16,768]{2,1,0:T(8,128)(2,1)} %bitcast.30), calls=%async_computation.1 | async-start | bytes 3145728 | tf_op jit(solution)/shard_map/all_to_all | solution.py:55
  37.7 51.8 %all-reduce.3.cloned.1.call-start = ((), (), s32[]{:S(2)}) async-start(), calls=%async_computation.3 | async-start | bytes 786432 | tf_op jit(solution)/shard_map/psum | solution.py:73
  39.7 101.9 %all-reduce.5.cloned.1.call-start = ((), (), s32[]{:S(2)}) async-start(), calls=%async_computation.4 | async-start | bytes 786432 | tf_op jit(solution)/shard_map/psum | solution.py:81
  89.5 1.8 copy-start.1
  92.3 1.2 copy-start.5
  93.5 76.0 %reduce-scatter.2.cloned.1.call-start = ((), (), s32[]{:S(2)}) async-start(), calls=%async_computation.5 | async-start | bytes 491520 | tf_op jit(solution)/shard_map/reduce_scatter | solution.py:88
  141.6 1.7 copy-start.2
  144.1 27.6 %copy-start.3 = (f32[32,1024]{1,0:T(8,128)}, f32[32,1024]{1,0:T(8,128)S(1)}, u32[]{:S(2)}) copy-start(f32[32,1024]{1,0:T(8,128)S(1)} %select_reduce_fusion.2) | copy-start | bytes 393220
Sparse Core Ops, SparseCore 0:
  40.8 48.6 all-reduce.2
  93.6 47.9 all-reduce.4
  145.4 24.1 reduce-scatter.1
where the time goes:
time: 179 us; the launch traced here: 178 us
  waiting for transfers between devices  116 us (65%)
  starting transfers between devices  17.9 us (10%)
  between operations  13.9 us (8%)
  matrix products  11.6 us (6%)
  blocking collectives  9.33 us (5%)
  other arithmetic  5.17 us (3%)
  local copies, waits for them, and re-layouts  3.95 us (2%)
    psum x1, waiting for transfers between devices, shards(): lead = lax.psum(jnp.dot(spread, points, preferred_element_type=F32), 'help')  48.3 us
    psum x1, waiting for transfers between devices, shards(): back, queried = lax.psum((back, named), 'help')  38.5 us
    reduce_scatter x1, waiting for transfers between devices, shards(): lax.psum_scatter(summed.reshape(clusters, rank, width), 'help', scatter_d...  23.7 us
    all_to_all x1, starting transfers between devices, shards(): lax.all_to_all(ids.astype(jnp.int32).reshape(groups, 1, capacity), 'shard...  12.1 us
    psum x1, blocking collectives, shards(): back, queried = lax.psum((back, named), 'help')  9.33 us
    all_to_all x1, waiting for transfers between devices, shards(): lax.all_to_all(ids.astype(jnp.int32).reshape(groups, 1, capacity), 'shard...  5.79 us
    all_to_all x1, starting transfers between devices, shards(): lax.all_to_all(packed.reshape(groups, capacity, width), 'shard', split_ax...  5.7 us
    dot_general x3, matrix products, dot2(): lax.dot_general(hi, w, (dims, ((), ())), preferred_element_type=F32)  3.8 us
  transfers between devices with their start and end apart: 5, of which 4 were waited for; matrix products, arithmetic and copies ran while one was open for 4% of the time, Pallas kernels for 0%

commit v1 on v0

--- a/solution.py
+++ b/solution.py
@@ -70,7 +70,9 @@
     spread = jnp.where(own_hot[:, None, :], test_matrix[None], 0).reshape(
         clusters * rank, own_points
     )
-    lead = lax.psum(jnp.dot(spread, points, preferred_element_type=F32), "help")
+    lead = jnp.sum(
+        lax.all_gather(jnp.dot(spread, points, preferred_element_type=F32), "help"), axis=0
+    )
     lifted = dot2(lead * scale, pool, ((1,), (1,)))
     pool_hot = pool_ids[None, :] == labels[:, None]
     lifted = jnp.where(pool_hot[:, None, :], lifted.reshape(clusters, rank, slots), 0.0).reshape(

time: 179 us -> 162 us (0.905)
  waiting for transfers between devices: 116 us -> 97.8 us
    psum x1 -> x0, waiting for transfers between devices: 48.3 us -> none  [shards(): lead = lax.psum(jnp.dot(spread, points, preferred_element_type=F32), 'help')]
    all_gather x0 -> x1, waiting for transfers between devices: none -> 30 us  [shards(): lax.all_gather(jnp.dot(spread, points, preferred_element_type=F32), 'help')]
    all_to_all x1, waiting for transfers between devices: 0.01 us -> 5.76 us  [shards(): lax.all_to_all(packed.reshape(groups, capacity, width), 'shard', split_ax...]
    psum x1, waiting for transfers between devices: 38.5 us -> 33 us  [shards(): back, queried = lax.psum((back, named), 'help')]
  transfers between devices with their start and end apart: 5 -> 5, of which waited for: 4 -> 5; matrix products, arithmetic and copies ran while one was open for 4% -> 5% of each run, Pallas kernels for 0% -> 0%
where the time goes in v1:
time: 162 us; the launch traced here: 161 us
  waiting for transfers between devices  97.8 us (60%)
  starting transfers between devices  17.9 us (11%)
  between operations  13.9 us (9%)
  matrix products  10.5 us (6%)
  blocking collectives  10.5 us (6%)
  other arithmetic  6.7 us (4%)
  local copies, waits for them, and re-layouts  3.94 us (2%)
    psum x1, waiting for transfers between devices, shards(): back, queried = lax.psum((back, named), 'help')  33 us
    all_gather x1, waiting for transfers between devices, shards(): lax.all_gather(jnp.dot(spread, points, preferred_element_type=F32), 'help')  30 us
    reduce_scatter x1, waiting for transfers between devices, shards(): lax.psum_scatter(summed.reshape(clusters, rank, width), 'help', scatter_d...  23.8 us
    all_to_all x1, starting transfers between devices, shards(): lax.all_to_all(ids.astype(jnp.int32).reshape(groups, 1, capacity), 'shard...  12.1 us
    psum x1, blocking collectives, shards(): back, queried = lax.psum((back, named), 'help')  10.5 us
    all_to_all x1, waiting for transfers between devices, shards(): lax.all_to_all(packed.reshape(groups, capacity, width), 'shard', split_ax...  5.76 us
    all_to_all x1, starting transfers between devices, shards(): lax.all_to_all(packed.reshape(groups, capacity, width), 'shard', split_ax...  5.7 us
    all_to_all x1, waiting for transfers between devices, shards(): lax.all_to_all(ids.astype(jnp.int32).reshape(groups, 1, capacity), 'shard...  5.1 us
  transfers between devices with their start and end apart: 5, of which 5 were waited for; matrix products, arithmetic and copies ran while one was open for 5% of the time, Pallas kernels for 0%

profile of v1, /device:TPU:8, one launch (start us, length us, event | category | flops | bytes accessed | tf_op | source)
XLA Modules:
  0.0 161.2 jit_solution(10040866281215919774)
XLA Ops:
  7.2 0.9 copy.22
  8.1 0.1 eq.103
  8.3 0.3 fusion.4
  8.6 0.1 convert_element_type.64
  8.8 0.7 multiply_add_fusion
  9.5 0.8 slice_add_fusion
  10.3 0.3 select_reduce_fusion
  10.6 0.7 add.89
  11.3 12.1 %all-to-all-start = ((s32[64,1,16]{2,1,0:T(1,128)}), s32[64,1,16]{2,1,0:T(1,128)S(1)}, u32[]{:S(2)}, u32[]{:S(2)}) async-start(s32[64,1,16]{2,1,0:T(1,128)} %bitcast.5), calls=%async_computation | async-start | bytes 65536 | tf_op jit(solution)/shard_map/all_to_all | solution.py:58
  23.4 2.8 %convolution_convert_fusion = bf16[1024,768]{1,0:T(8,128)(2,1)} fusion(bf16[256,768]{1,0:T(8,128)(2,1)} %param.6, s32[256]{0:T(256)S(1)} %bitcast.40, s32[256]{0:T(256)S(1)} %bitcast.38), kind=kOutput, calls=%fused_computation | convolution fusion | flops 404226048 | bytes 1968128 | tf_op jit(solution)/shard_map/dot_general | solution.py:46
  26.2 0.7 constant_dynamic-slice_fusion
  26.9 5.1 %all-to-all-done = s32[64,1,16]{2,1,0:T(1,128)S(1)} async-done(((s32[64,1,16]{2,1,0:T(1,128)}), s32[64,1,16]{2,1,0:T(1,128)S(1)}, u32[]{:S(2)}, u32[]{:S(2)}) %all-to-all-start) | async-done | bytes 4128 | tf_op jit(solution)/shard_map/all_to_all | solution.py:58
  32.0 5.7 %all-to-all-start.1 = ((bf16[64,16,768]{2,1,0:T(8,128)(2,1)}), bf16[64,16,768]{2,1,0:T(8,128)(2,1)S(1)}, u32[]{:S(2)}, u32[]{:S(2)}) async-start(bf16[64,16,768]{2,1,0:T(8,128)(2,1)} %bitcast.31), calls=%async_computation.1 | async-start | bytes 3145728 | tf_op jit(solution)/shard_map/all_to_all | solution.py:55
  37.8 1.1 fusion.29
  39.0 0.5 broadcast.69
  39.5 0.7 reduce.3
  40.5 30.0 %all-gather.3.cloned.1.call-done = f32[512,768]{1,0:T(8,128)} async-done(((f32[128,768]{1,0:T(8,128)}), f32[512,768]{1,0:T(8,128)}) %all-gather.3.cloned.1.call-update) | async-done | bytes 1572880 | tf_op jit(solution)/shard_map/all_gather | solution.py:74
  70.5 1.5 reduce_sum.66
  72.0 5.8 %all-to-all-done.1 = bf16[64,16,768]{2,1,0:T(8,128)(2,1)S(1)} async-done(((bf16[64,16,768]{2,1,0:T(8,128)(2,1)}), bf16[64,16,768]{2,1,0:T(8,128)(2,1)S(1)}, u32[]{:S(2)}, u32[]{:S(2)}) %all-to-all-start.1) | async-done | bytes 1572896 | tf_op jit(solution)/shard_map/all_to_all | solution.py:55
  77.8 0.6 fusion.9
  78.5 0.7 fusion.3
  79.1 0.4 fusion.16
  79.6 1.1 convolution_add_fusion.2
  80.8 0.1 convert_reduce_fusion
  80.9 10.5 %psum.15 = f32[4]{0:T(128)S(1)} all-reduce(f32[4]{0:T(128)S(1)} %get-tuple-element.2), channel_id=1, replica_groups=mesh['shard'=64,'help'=4] {'help'}, use_global_device_ids=true, to_apply=%region_6.7 | all-reduce | flops 4 | bytes 32 | tf_op jit(solution)/shard_map/psum | solution.py:83
  91.4 33.0 %all-reduce.2.cloned.1.call-done = f32[128,768]{1,0:T(8,128)} async-done(((f32[128,768]{1,0:T(8,128)}), f32[128,768]{1,0:T(8,128)}) %all-reduce.2.cloned.1.call-update) | async-done | bytes 393232 | tf_op jit(solution)/shard_map/psum | solution.py:83
  124.5 1.7 %fusion.21 = f32[128,1024]{1,0:T(8,128)S(1)} fusion(bf16[1024,768]{1,0:T(8,128)(2,1)S(1)} %copy-done, f32[128,768]{1,0:T(8,128)} %all-reduce.2.cloned.1.call-done), kind=kOutput, calls=%fused_computation.37 | convolution fusion | flops 201424896 | bytes 2490368 | tf_op jit(solution)/shard_map/dot_general | solution.py:18
  126.2 0.7 convolution_add_fusion
  127.0 1.1 fusion
  128.2 0.6 dynamic_slice.7
  128.8 23.8 %reduce-scatter.2.cloned.1.call-done = f32[1,32,768]{2,1,0:T(8,128)} async-done(((f32[4,32,768]{2,1,0:T(8,128)}), f32[1,32,768]{2,1,0:T(8,128)}) %reduce-scatter.2.cloned.1.call-update) | async-done | bytes 98320 | tf_op jit(solution)/shard_map/reduce_scatter | solution.py:90
  152.5 2.2 %broadcast_multiply_fusion = f32[1,32,768]{2,1,0:T(8,128)} fusion(f32[1,32,768]{2,1,0:T(8,128)} %reduce-scatter.2.cloned.1.call-done, f32[]{:T(128)} %bitcast.14), kind=kLoop, calls=%fused_computation.42 | loop fusion | flops 24576 | bytes 196612 | tf_op jit(solution)/shard_map/mul | solution.py:94
  (28 shorter events, 0.7 us)
Async XLA Ops:
  7.2 30.6 %copy-start = (bf16[1024,768]{1,0:T(8,128)(2,1)S(1)}, bf16[1024,768]{1,0:T(8,128)(2,1)}, u32[]{:S(2)}) copy-start(bf16[1024,768]{1,0:T(8,128)(2,1)} %param.9) | copy-start | bytes 4718596
  11.3 20.7 %all-to-all-start = ((s32[64,1,16]{2,1,0:T(1,128)}), s32[64,1,16]{2,1,0:T(1,128)S(1)}, u32[]{:S(2)}, u32[]{:S(2)}) async-start(s32[64,1,16]{2,1,0:T(1,128)} %bitcast.5), calls=%async_computation | async-start | bytes 65536 | tf_op jit(solution)/shard_map/all_to_all | solution.py:58
  32.0 5.8 %copy-start.3 = (bf16[32,1024]{1,0:T(8,128)(2,1)S(1)}, bf16[32,1024]{1,0:T(8,128)(2,1)}, u32[]{:S(2)}) copy-start(bf16[32,1024]{1,0:T(8,128)(2,1)} %param.11) | copy-start | bytes 196612
  32.0 45.8 %all-to-all-start.1 = ((bf16[64,16,768]{2,1,0:T(8,128)(2,1)}), bf16[64,16,768]{2,1,0:T(8,128)(2,1)S(1)}, u32[]{:S(2)}, u32[]{:S(2)}) async-start(bf16[64,16,768]{2,1,0:T(8,128)(2,1)} %bitcast.31), calls=%async_computation.1 | async-start | bytes 3145728 | tf_op jit(solution)/shard_map/all_to_all | solution.py:55
  37.7 32.8 %all-gather.3.cloned.1.call-start = ((), (), s32[]{:S(2)}) async-start(), calls=%async_computation.5 | async-start | bytes 1966080 | tf_op jit(solution)/shard_map/all_gather | solution.py:74
  39.0 85.5 %all-reduce.2.cloned.1.call-start = ((), (), s32[]{:S(2)}) async-start(), calls=%async_computation.3 | async-start | bytes 786432 | tf_op jit(solution)/shard_map/psum | solution.py:83
  79.5 1.2 copy-start.4
  80.7 71.8 %reduce-scatter.2.cloned.1.call-start = ((), (), s32[]{:S(2)}) async-start(), calls=%async_computation.4 | async-start | bytes 491520 | tf_op jit(solution)/shard_map/reduce_scatter | solution.py:90
  124.5 1.7 %copy-start.1 = (f32[128,768]{1,0:T(8,128)S(1)}, f32[128,768]{1,0:T(8,128)}, u32[]{:S(2)}) copy-start(f32[128,768]{1,0:T(8,128)} %all-reduce.2.cloned.1.call-done) | copy-start | bytes 1179652
  127.0 27.7 %copy-start.2 = (f32[32,1024]{1,0:T(8,128)}, f32[32,1024]{1,0:T(8,128)S(1)}, u32[]{:S(2)}) copy-start(f32[32,1024]{1,0:T(8,128)S(1)} %select_reduce_fusion.2) | copy-start | bytes 393220
Sparse Core Ops, SparseCore 0:
  40.3 30.1 all-gather.2
  80.8 43.5 all-reduce.1
  128.3 24.2 reduce-scatter.1
